TPU v7x, 128 devices: a whole 4x4x4 slice. The times are simulated.
128 devices in a mesh: half: 2 (over y_hi), row: 8 (over y_lo, z), col: 8 (over x, core).
Axes of the slice: x: 4, y: 4 (y_hi: 2, y_lo: 2; y = y_hi * 2 + y_lo), z: 4, core: 2. Of those that a mesh axis runs over, the one named last changes fastest.
Arguments:
- child_block: bfloat16 [2, 8, 8, 256, 8, 8, 256], P('half', None, 'row', None, None, 'col'), may hold values from -6 to 6
- child_row: bfloat16 [2, 256, 8, 8, 256], P('half', 'row', None, 'col'), may hold values from -6 to 6
- child_col: bfloat16 [2, 256, 8, 8, 256], P('half', 'col', None, 'row'), may hold values from -0.375 to 0.375
- child_pivot_inv: bfloat16 [2, 256, 256], P('half'), may hold values from -0.375 to 0.375
- child_map: int32 [2, 64], replicated, may hold values from 0 to 126, as said below
- parent_row: bfloat16 [256, 8, 16, 256], P('row', None, ('half', 'col')), may hold values from -6 to 6
- parent_col: bfloat16 [256, 16, 8, 256], P(('half', 'col'), None, 'row'), may hold values from -0.375 to 0.375
- parent_pivot_inv: bfloat16 [256, 256], replicated, may hold values from -0.375 to 0.375
- parent_diag: float32 [16, 8, 256], P(None, 'row'), may hold values from 1 to 3
Outputs:
- schur: bfloat16 [16, 8, 256, 8, 16, 256], P(None, 'row', None, None, ('half', 'col'))
Inputs may be any that keep to these rules, and one draw needn't show every extreme that they name: child_map[h, 8 * k + r] = 2 * 8 * k + r + p_h[k] for k and r from 0 to 7, where p_0 and p_1 are permutations of 0 to 7.
All inputs are finite; a program needn't handle non-finite values.
Results may differ from a plain program's by a relative error of at most 0.0041.
The roundings to bfloat16 on the way count: a program that leaves them out, or rounds other values in their place, can miss the bound.
Values may be sent and summed in bfloat16 or wider, within the bound.
A program may use at most 384 MiB of HBM per device.

v0:
```python
import jax
import jax.numpy as jnp
from jax import lax
from jax.sharding import PartitionSpec as P


def inverse_maps(child_map, parent_tiles):
    targets = jnp.arange(parent_tiles, dtype=jnp.int32)
    matches = child_map[:, None, :] == targets[None, :, None]
    covered = jnp.any(matches, axis=2)
    positions = jnp.arange(child_map.shape[1], dtype=jnp.int32)
    sources = jnp.sum(jnp.where(matches, positions[None, None, :], 0), axis=2)
    return (covered, sources)


def pick_index(keys, wanted):
    positions = jnp.arange(keys.shape[0], dtype=jnp.int32)
    matched = keys[None, :] == wanted[:, None]
    return (jnp.sum(jnp.where(matched, positions[None, :], 0), axis=1), jnp.any(matched, axis=1))


def shards(
    child_block,
    child_row,
    child_col,
    child_pivot_inv,
    child_map,
    parent_row,
    parent_col,
    parent_pivot_inv,
    parent_diag,
):
    grid_size = lax.axis_size("row")
    tile_width = child_pivot_inv.shape[-1]
    my_half = lax.axis_index("half")
    my_row = lax.axis_index("row")
    my_col = lax.axis_index("col")
    local_width = grid_size * tile_width
    parent_height = 2 * grid_size * tile_width
    child_inv = child_pivot_inv[0]
    pieces = (
        lax.all_gather(child_row[0], "row", axis=0, tiled=True),
        lax.all_gather(parent_row, "row", axis=0, tiled=True),
    )
    piece_rows = pieces[0].shape[0]
    child_piece = pieces[0].reshape(piece_rows, local_width)
    parent_piece = pieces[1].reshape(piece_rows, local_width)
    child_sum = jnp.dot(child_inv, child_piece, preferred_element_type=jnp.float32)
    parent_sum = jnp.dot(parent_pivot_inv, parent_piece, preferred_element_type=jnp.float32)
    child_scaled = child_sum
    parent_scaled = parent_sum
    child_scaled = child_scaled.astype(jnp.bfloat16)
    parent_scaled = parent_scaled.astype(jnp.bfloat16)
    piece = lax.all_gather(child_col, "col", axis=1, tiled=True)
    piece_rows = piece.shape[1]
    flattened = piece.reshape(piece_rows, local_width)
    scaled_part = child_scaled
    child_update = lax.dot_general(
        flattened, scaled_part, (((0,), (0,)), ((), ())), preferred_element_type=jnp.float32
    )
    contribution = (
        child_block.reshape(local_width, local_width).astype(jnp.float32) - child_update
    ).astype(jnp.bfloat16)
    tile_grid = contribution.reshape(grid_size, tile_width, grid_size, tile_width)
    parent_rows = grid_size * jnp.arange(2 * grid_size, dtype=jnp.int32) + my_row
    column_slot = my_half * grid_size + my_col
    parent_columns = 2 * grid_size * jnp.arange(grid_size, dtype=jnp.int32) + column_slot
    diag_values = parent_diag.reshape(2 * grid_size, tile_width)
    on_diagonal = (parent_rows[:, None] == parent_columns[None, :]).astype(jnp.float32)
    identity = jnp.eye(tile_width, dtype=jnp.float32)
    diag_term = (
        diag_values[:, :, None, None] * on_diagonal[:, None, :, None] * identity[None, :, None, :]
    ).reshape(parent_height, local_width)
    piece = lax.all_gather(parent_col, ("half", "col"), axis=0, tiled=True)
    piece_rows = piece.shape[0]
    flattened = piece.reshape(piece_rows, parent_height)
    scaled_part = parent_scaled
    parent_front = diag_term - lax.dot_general(
        flattened, scaled_part, (((0,), (0,)), ((), ())), preferred_element_type=jnp.float32
    )
    covered, sources = inverse_maps(child_map, 2 * grid_size * grid_size)
    own_map = jnp.take(child_map, my_half, axis=0).reshape(grid_size, grid_size)
    row_targets = lax.dynamic_index_in_dim(own_map, my_row, 1, keepdims=False)
    col_targets = lax.dynamic_index_in_dim(own_map, my_col, 1, keepdims=False)
    slots_small = jnp.arange(grid_size, dtype=jnp.int32)
    row_pick, row_found = pick_index(row_targets % grid_size, slots_small)
    row_covered = covered[:, parent_rows]
    row_source = sources[:, parent_rows] % grid_size
    col_covered = covered[:, parent_columns]
    col_source = sources[:, parent_columns] % grid_size
    usable = row_covered[:, :, None] & col_covered[:, None, :]
    by_rows = jnp.take(tile_grid, row_pick, axis=0)
    column_slots = jnp.arange(2 * grid_size, dtype=jnp.int32)
    col_pick, col_live = pick_index(col_targets % (2 * grid_size), column_slots)
    packed = jnp.take(by_rows, col_pick, axis=2)
    packed = jnp.where(col_live[None, None, :, None], packed, jnp.zeros((), jnp.bfloat16))
    moved_rows = lax.all_to_all(packed, "row", split_axis=0, concat_axis=0, tiled=True)
    arrived = lax.all_to_all(moved_rows, ("half", "col"), split_axis=2, concat_axis=2, tiled=True)
    sibling_pieces = []
    for sibling in range(2):
        picked = jnp.take(arrived, row_source[sibling], axis=0)
        sibling_pieces.append(jnp.take(picked, sibling * grid_size + col_source[sibling], axis=2))
    front_blocks = parent_front.reshape(2 * grid_size, tile_width, grid_size, tile_width)
    for sibling in range(2):
        mask = usable[sibling][:, None, :, None]
        front_blocks = front_blocks + jnp.where(
            mask, sibling_pieces[sibling].astype(jnp.float32), 0.0
        )
    schur_front = front_blocks.astype(jnp.bfloat16)
    return schur_front.reshape(2 * grid_size, 1, tile_width, grid_size, 1, tile_width)


def solution(mesh):
    return jax.shard_map(
        shards,
        mesh=mesh,
        in_specs=(
            P("half", None, "row", None, None, "col", None),
            P("half", "row", None, "col", None),
            P("half", "col", None, "row", None),
            P("half", None, None),
            P(),
            P("row", None, ("half", "col"), None),
            P(("half", "col"), None, "row", None),
            P(),
            P(None, "row", None),
        ),
        out_specs=P(None, "row", None, None, ("half", "col"), None),
        check_vma=False,
    )
```

profile of v0, /device:TPU:1, one launch (start us, length us, event | category | flops | bytes accessed | tf_op | source)
XLA Modules:
  0.0 912.3 jit_solution(1902297807044894404)
XLA Ops:
  8.8 13.8 %copy.75 = f32[256,8,8,256]{3,1,2,0:T(8,128)} copy(bf16[256,8,8,256]{3,2,1,0:T(8,128)(2,1)} %bitcast.101) | data formatting | bytes 25165824
  22.6 18.1 %copy.67 = f32[2048,2048]{0,1:T(8,128)} copy(f32[2048,2048]{1,0:T(8,128)} %bitcast.94) | data formatting | bytes 33554432 | tf_op jit(solution)/shard_map/convert_element_type | solution.py:62
  47.6 28.0 %all-gather.10.cloned.1.call-done = bf16[1,256,8,1,256]{4,2,3,0,1:T(8,128)(2,1)} async-done(((bf16[1,32,8,1,256]{4,2,3,0,1:T(8,128)(2,1)}), bf16[1,256,8,1,256]{4,2,3,0,1:T(8,128)(2,1)}) %all-gather.10.cloned.1.call-update) | async-done | bytes 1048592 | tf_op jit(solution)/shard_map/all_gather | solution.py:54
  96.7 12.6 %copy.58 = bf16[8,256,8,256]{3,1,2,0:T(8,128)(2,1)} copy(bf16[8,256,8,256]{1,0,3,2:T(8,128)(2,1)} %bitcast.100) | data formatting | bytes 16777216 | tf_op jit(solution)/shard_map/reshape | solution.py:64
  124.8 10.7 %gather_fusion.3 = bf16[16,8,256,256]{3,2,1,0:T(8,128)(2,1)} fusion(bf16[8,256,8,256]{3,1,2,0:T(8,128)(2,1)} %broadcast_select_fusion, s32[1024]{0:T(1024)S(1)} %pad_clamp_fusion.4), kind=kCustom, calls=%fused_computation.11 | custom fusion | bytes 33554496 | tf_op jit(solution)/shard_map/jit(_take)/gather | solution.py:95
  146.5 187.8 %all_to_all.10 = bf16[8,256,16,256]{3,1,2,0:T(8,128)(2,1)S(1)} all-to-all(bf16[8,256,16,256]{3,1,2,0:T(8,128)(2,1)S(1)} %copy.59), channel_id=1, replica_groups=mesh['half'=2,'row'=8,'col'=8] {'row'}, dimensions={0} | all-to-all | bytes 33554432 | tf_op jit(solution)/shard_map/all_to_all | solution.py:97
  357.2 36.2 %copy.71 = f32[256,8,16,256]{3,1,2,0:T(8,128)} copy(f32[256,8,16,256]{3,2,1,0:T(8,128)S(1)} %bitcast.92) | data formatting | bytes 67108864
  396.8 93.5 %all-gather.6.cloned.1.call-done = bf16[256,8,1,256]{3,1,2,0:T(8,128)(2,1)} async-done(((bf16[32,8,1,256]{3,1,2,0:T(8,128)(2,1)}), bf16[256,8,1,256]{3,1,2,0:T(8,128)(2,1)}) %all-gather.6.cloned.1.call-update) | async-done | bytes 1048592 | tf_op jit(solution)/shard_map/all_gather | solution.py:43
  491.9 88.7 %all-gather.8.cloned.1.call-done = bf16[256,16,1,256]{3,1,2,0:T(8,128)(2,1)} async-done(((bf16[16,16,1,256]{3,1,2,0:T(8,128)(2,1)}), bf16[256,16,1,256]{3,1,2,0:T(8,128)(2,1)}) %all-gather.8.cloned.1.call-update) | async-done | bytes 2097168 | tf_op jit(solution)/shard_map/all_gather | solution.py:74
  583.1 21.5 %bitcast_subtract_fusion = f32[4096,2048]{0,1:T(8,128)} fusion(f32[4096,2048]{0,1:T(8,128)} %bitcast.90, bf16[256,4096]{1,0:T(8,128)(2,1)S(1)} %bitcast.102, bf16[256,256]{1,0:T(8,128)(2,1)S(1)} %copy-done, bf16[256,2048]{1,0:T(8,128)(2,1)S(1)} %bitcast.103), kind=kOutput, calls=%fused_computation.16 | convolution fusion | flops 4572315648 | bytes 70385664 | tf_op jit(solution)/shard_map/dot_general | solution.py:78
  604.5 30.2 %copy.74 = f32[256,8,16,256]{3,2,1,0:T(8,128)} copy(f32[256,8,16,256]{3,1,2,0:T(8,128)} %bitcast.91) | data formatting | bytes 67108864
  634.7 34.4 %copy.63 = f32[16,256,8,256]{3,1,0,2:T(8,128)} copy(f32[16,256,8,256]{1,0,3,2:T(8,128)} %bitcast.93) | data formatting | bytes 67108864 | tf_op jit(solution)/shard_map/reshape | solution.py:103
  669.2 12.0 %fusion.18 = (bf16[8,128,16,256]{3,1,0,2:T(8,128)(2,1)}, bf16[8,128,16,256]{3,1,0,2:T(8,128)(2,1)}) fusion(bf16[8,256,16,256]{3,1,0,2:T(8,128)(2,1)} %all-to-all-done.1), kind=kLoop, calls=%fused_computation.102 | loop fusion | bytes 33554432 | tf_op jit(solution)/shard_map/jit(_take)/gather | solution.py:101
  696.6 10.5 %gather_fusion.11 = bf16[16,128,16,256]{3,1,2,0:T(8,128)(2,1)} fusion(bf16[8,128,16,256]{3,1,2,0:T(8,128)(2,1)} %copy.70, s32[1024]{0:T(1024)S(1)} %pad_clamp_fusion.1), kind=kCustom, calls=%fused_computation.5.clone | custom fusion | bytes 33554496 | tf_op jit(solution)/shard_map/jit(_take)/gather | solution.py:101
  707.1 10.6 %gather_fusion.7 = bf16[16,128,16,256]{3,1,2,0:T(8,128)(2,1)} fusion(bf16[8,128,16,256]{3,1,2,0:T(8,128)(2,1)} %copy.70, s32[1024]{0:T(1024)S(1)} %pad_clamp_fusion.3), kind=kCustom, calls=%fused_computation.1.clone | custom fusion | bytes 33554496 | tf_op jit(solution)/shard_map/jit(_take)/gather | solution.py:101
  728.1 10.5 %gather_fusion.10 = bf16[16,128,16,256]{3,1,2,0:T(8,128)(2,1)} fusion(bf16[8,128,16,256]{3,1,2,0:T(8,128)(2,1)} %copy.69, s32[1024]{0:T(1024)S(1)} %pad_clamp_fusion.1), kind=kCustom, calls=%fused_computation.4.clone | custom fusion | bytes 33554496 | tf_op jit(solution)/shard_map/jit(_take)/gather | solution.py:101
  738.6 22.6 %maximum_select_fusion = bf16[16,256,16,256]{3,1,2,0:T(8,128)(2,1)} fusion(bf16[16,128,16,256]{3,1,2,0:T(8,128)(2,1)} %gather_fusion.7, bf16[16,128,16,256]{3,1,2,0:T(8,128)(2,1)} %gather_fusion.6, pred[16]{0:T(512)(128)(4,1)S(1)} %get-tuple-element.39), kind=kLoop, calls=%fused_computation.14 | loop fusion | flops 83886080 | bytes 67108880 | tf_op jit(solution)/shard_map/jit(_take)/select_n | solution.py:101
  761.3 23.3 %fusion.17 = (bf16[16,128,16,256]{3,1,2,0:T(8,128)(2,1)}, bf16[16,128,16,256]{3,1,2,0:T(8,128)(2,1)}) fusion(bf16[16,256,16,256]{3,1,2,0:T(8,128)(2,1)} %maximum_select_fusion), kind=kLoop, calls=%fused_computation.101 | loop fusion | bytes 67108864 | tf_op jit(solution)/shard_map/jit(_take)/gather | solution.py:102
  794.9 10.4 %gather_fusion.9 = bf16[8,16,128,256]{3,2,1,0:T(8,128)(2,1)} fusion(bf16[16,128,16,256]{3,1,2,0:T(8,128)(2,1)} %get-tuple-element.27, s32[1024]{0:T(1024)} %pad_clamp_fusion.2), kind=kCustom, calls=%fused_computation.3.clone | custom fusion | bytes 16777248 | tf_op jit(solution)/shard_map/jit(_take)/gather | solution.py:102
  805.4 22.6 %maximum_select_fusion.1 = bf16[16,256,16,256]{3,1,2,0:T(8,128)(2,1)} fusion(bf16[16,128,16,256]{3,1,2,0:T(8,128)(2,1)} %gather_fusion.11, bf16[16,128,16,256]{3,1,2,0:T(8,128)(2,1)} %gather_fusion.10, pred[16]{0:T(512)(128)(4,1)S(1)} %copy-done.9), kind=kLoop, calls=%fused_computation.15 | loop fusion | flops 83886080 | bytes 67108880 | tf_op jit(solution)/shard_map/jit(_take)/select_n | solution.py:101
  828.0 23.3 %fusion.16 = (bf16[16,128,16,256]{3,1,2,0:T(8,128)(2,1)}, bf16[16,128,16,256]{3,1,2,0:T(8,128)(2,1)}) fusion(bf16[16,256,16,256]{3,1,2,0:T(8,128)(2,1)} %maximum_select_fusion.1), kind=kLoop, calls=%fused_computation.100 | loop fusion | bytes 67108864 | tf_op jit(solution)/shard_map/jit(_take)/gather | solution.py:102
  861.7 10.5 %gather_fusion.13 = bf16[8,16,128,256]{3,2,1,0:T(8,128)(2,1)} fusion(bf16[16,128,16,256]{3,1,2,0:T(8,128)(2,1)} %get-tuple-element.25, s32[1024]{0:T(1024)} %pad_clamp_fusion), kind=kCustom, calls=%fused_computation.7.clone | custom fusion | bytes 16777248 | tf_op jit(solution)/shard_map/jit(_take)/gather | solution.py:102
  872.3 22.2 %fusion = bf16[16,1,256,8,1,256]{5,2,0,3,4,1:T(8,128)(2,1)S(1)} fusion(f32[16,256,8,256]{3,1,0,2:T(8,128)} %copy.63, bf16[16,128,8,256]{3,1,0,2:T(8,128)(2,1)} %bitcast.96, bf16[16,128,8,256]{3,1,0,2:T(8,128)(2,1)} %bitcast.95, bf16[16,128,8,256]{3,1,0,2:T(8,128)(2,1)} %bitcast.98, bf16[16,128,8,256]{3,1,0,2:T(8,128)(2,1)} %bitcast.97, ...), kind=kLoop, calls=%fused_computation.18 | loop fusion | flops 142606336 | bytes 83886352 | tf_op jit(solution)/shard_map/reshape | solution.py:110
  894.5 11.1 %copy.66 = bf16[16,1,256,8,1,256]{5,3,4,2,1,0:T(8,128)(2,1)} copy(bf16[16,1,256,8,1,256]{5,2,0,3,4,1:T(8,128)(2,1)S(1)} %fusion) | data formatting | bytes 33554432 | tf_op jit(solution)/shard_map/reshape | solution.py:110
  (95 shorter events, 133.4 us)
Async XLA Ops:
  6.5 576.5 %copy-start = (bf16[256,256]{1,0:T(8,128)(2,1)S(1)}, bf16[256,256]{1,0:T(8,128)(2,1)}, u32[]{:S(2)}) copy-start(bf16[256,256]{1,0:T(8,128)(2,1)} %param.20) | copy-start | bytes 393220
  6.5 39.5 %all-gather.12.cloned.1.call-start = ((), (), s32[]{:S(2)}) async-start(), calls=%async_computation.5 | async-start | bytes 1179648 | tf_op jit(solution)/shard_map/all_gather | solution.py:42
  7.3 68.3 %all-gather.10.cloned.1.call-start = ((), (), s32[]{:S(2)}) async-start(), calls=%async_computation.4 | async-start | bytes 1179648 | tf_op jit(solution)/shard_map/all_gather | solution.py:54
  22.6 54.5 %copy-start.2 = (bf16[1,256,256]{2,1,0:T(8,128)(2,1)S(1)}, bf16[1,256,256]{2,1,0:T(8,128)(2,1)}, u32[]{:S(2)}) copy-start(bf16[1,256,256]{2,1,0:T(8,128)(2,1)} %param.16) | copy-start | bytes 393220
  340.8 8.7 copy-start.6
  340.8 11.6 %copy-start.3 = (f32[16,1,256]{2,1,0:T(1,128)S(1)}, f32[16,1,256]{2,1,0:T(1,128)}, u32[]{:S(2)}) copy-start(f32[16,1,256]{2,1,0:T(1,128)} %param.21) | copy-start | bytes 49156
  340.8 328.4 %all-to-all-start.1 = ((bf16[8,256,16,256]{3,1,0,2:T(8,128)(2,1)}), bf16[8,256,16,256]{3,1,0,2:T(8,128)(2,1)}, u32[]{:S(2)}, u32[]{:S(2)}) async-start(bf16[8,256,16,256]{3,1,0,2:T(8,128)(2,1)} %copy.60), calls=%async_computation.1 | async-start | bytes 33554432 | tf_op jit(solution)/shard_map/all_to_all | solution.py:98
  348.1 142.2 %all-gather.6.cloned.1.call-start = ((), (), s32[]{:S(2)}) async-start(), calls=%async_computation.2 | async-start | bytes 1179648 | tf_op jit(solution)/shard_map/all_gather | solution.py:43
  348.9 231.7 %all-gather.8.cloned.1.call-start = ((), (), s32[]{:S(2)}) async-start(), calls=%async_computation.3 | async-start | bytes 2228224 | tf_op jit(solution)/shard_map/all_gather | solution.py:74
  784.6 20.8 %copy-start.9 = (pred[16]{0:T(512)(128)(4,1)S(1)}, pred[16]{0:T(512)(128)(4,1)}, u32[]{:S(2)}) copy-start(pred[16]{0:T(512)(128)(4,1)} %get-tuple-element.38) | copy-start | bytes 52
  851.4 20.9 %copy-start.4 = (pred[16,8]{0,1:T(8,128)(4,1)S(1)}, pred[16,8]{0,1:T(8,128)(4,1)}, u32[]{:S(2)}) copy-start(pred[16,8]{0,1:T(8,128)(4,1)} %get-tuple-element.30) | copy-start | bytes 388
  851.4 20.9 %copy-start.5 = (pred[16,8]{0,1:T(8,128)(4,1)S(1)}, pred[16,8]{0,1:T(8,128)(4,1)}, u32[]{:S(2)}) copy-start(pred[16,8]{0,1:T(8,128)(4,1)} %get-tuple-element.31) | copy-start | bytes 388
  851.4 20.9 %copy-start.7 = (pred[8]{0:T(512)(128)(4,1)S(1)}, pred[8]{0:T(512)(128)(4,1)}, u32[]{:S(2)}) copy-start(pred[8]{0:T(512)(128)(4,1)} %get-tuple-element.36) | copy-start | bytes 28
  851.4 20.9 %copy-start.8 = (pred[8]{0:T(512)(128)(4,1)S(1)}, pred[8]{0:T(512)(128)(4,1)}, u32[]{:S(2)}) copy-start(pred[8]{0:T(512)(128)(4,1)} %get-tuple-element.37) | copy-start | bytes 28
  872.3 33.3 %copy-start.1 = (bf16[256,256]{1,0:T(8,128)(2,1)S(1)}, bf16[256,256]{1,0:T(8,128)(2,1)}, u32[]{:S(2)}) copy-start(bf16[256,256]{1,0:T(8,128)(2,1)} %param.20) | copy-start | bytes 393220
Sparse Core Ops, SparseCore 0:
  9.0 37.0 all-gather.11
  47.8 27.7 all-gather.9
  350.6 139.6 all-gather.5
  492.6 87.8 all-gather.7
where the time goes:
time: 918 us; the launch traced here: 912 us
  local copies, waits for them, and re-layouts  363 us (40%)
  waiting for transfers between devices  218 us (24%)
  blocking collectives  188 us (20%)
  other arithmetic  92.2 us (10%)
  matrix products  30.8 us (3%)
  between operations  13.6 us (1%)
    all_to_all x1, blocking collectives, shards(): lax.all_to_all(packed, 'row', split_axis=0, concat_axis=0, tiled=True)  188 us
    unnamed x31, local copies, waits for them, and re-layouts  113 us
    all_gather x1, waiting for transfers between devices, shards(): lax.all_gather(parent_row, 'row', axis=0, tiled=True)  93.5 us
    all_gather x1, waiting for transfers between devices, shards(): piece = lax.all_gather(parent_col, ('half', 'col'), axis=0, tiled=True)  88.7 us
    gather x6, local copies, waits for them, and re-layouts, shards(): jnp.take(picked, sibling * grid_size + col_source[sibling], axis=2)  88.3 us
    gather x5, local copies, waits for them, and re-layouts, shards(): picked = jnp.take(arrived, row_source[sibling], axis=0)  54 us
    select_n x3, other arithmetic, shards(): picked = jnp.take(arrived, row_source[sibling], axis=0)  45.3 us
    reshape x1, local copies, waits for them, and re-layouts, shards(): parent_front.reshape(2 * grid_size, tile_width, grid_size, tile_width)  34.4 us
  transfers between devices with their start and end apart: 5, of which 4 were waited for; matrix products, arithmetic and copies ran while one was open for 19% of the time, Pallas kernels for 0%

commit v1 on v0

--- a/solution.py
+++ b/solution.py
@@ -71,7 +71,12 @@
     diag_term = (
         diag_values[:, :, None, None] * on_diagonal[:, None, :, None] * identity[None, :, None, :]
     ).reshape(parent_height, local_width)
-    piece = lax.all_gather(parent_col, ("half", "col"), axis=0, tiled=True)
+    piece = jnp.concatenate(
+        lax.all_to_all(
+            jnp.stack([parent_col] * lax.axis_size(("half", "col"))), ("half", "col"), 0, 0
+        ),
+        axis=0,
+    )
     piece_rows = piece.shape[0]
     flattened = piece.reshape(piece_rows, parent_height)
     scaled_part = parent_scaled

time: 918 us -> 863 us (0.940)
  waiting for transfers between devices: 218 us -> 135 us
  local copies, waits for them, and re-layouts: 363 us -> 375 us
    all_gather x1 -> x0, waiting for transfers between devices: 88.7 us -> none  [shards(): piece = lax.all_gather(parent_col, ('half', 'col'), axis=0, tiled=True)]
    all_to_all x0 -> x1, waiting for transfers between devices: none -> 14.5 us  [shards(): lax.all_to_all(jnp.stack([parent_col] * lax.axis_size(('half', 'col'))),...]
    unnamed x31 -> x35, local copies, waits for them, and re-layouts: 113 us -> 116 us
  transfers between devices with their start and end apart: 5 -> 5, of which waited for: 4 -> 4; matrix products, arithmetic and copies ran while one was open for 19% -> 23% of each run, Pallas kernels for 0% -> 0%
where the time goes in v1:
time: 863 us; the launch traced here: 854 us
  local copies, waits for them, and re-layouts  375 us (43%)
  blocking collectives  188 us (22%)
  waiting for transfers between devices  135 us (16%)
  other arithmetic  99.1 us (11%)
  matrix products  30.8 us (4%)
  between operations  13.6 us (2%)
  starting transfers between devices  12.9 us (1%)
    all_to_all x1, blocking collectives, shards(): lax.all_to_all(packed, 'row', split_axis=0, concat_axis=0, tiled=True)  188 us
    unnamed x35, local copies, waits for them, and re-layouts  116 us
    gather x6, local copies, waits for them, and re-layouts, shards(): jnp.take(picked, sibling * grid_size + col_source[sibling], axis=2)  88.3 us
    all_gather x1, waiting for transfers between devices, shards(): lax.all_gather(parent_row, 'row', axis=0, tiled=True)  85.6 us
    gather x5, local copies, waits for them, and re-layouts, shards(): picked = jnp.take(arrived, row_source[sibling], axis=0)  54 us
    select_n x3, other arithmetic, shards(): picked = jnp.take(arrived, row_source[sibling], axis=0)  45.3 us
    reshape x1, local copies, waits for them, and re-layouts, shards(): parent_front.reshape(2 * grid_size, tile_width, grid_size, tile_width)  34.6 us
    dot_general x2, matrix products, shards(): lax.dot_general(flattened, scaled_part, (((0,), (0,)), ((), ())), preferr...  30.8 us
  transfers between devices with their start and end apart: 5, of which 4 were waited for; matrix products, arithmetic and copies ran while one was open for 23% of the time, Pallas kernels for 0%

profile of v1, /device:TPU:1, one launch (start us, length us, event | category | flops | bytes accessed | tf_op | source)
XLA Modules:
  0.0 854.4 jit_solution(10321642685640710645)
XLA Ops:
  8.8 13.8 %copy.75 = f32[256,8,8,256]{3,1,2,0:T(8,128)} copy(bf16[256,8,8,256]{3,2,1,0:T(8,128)(2,1)} %bitcast.102) | data formatting | bytes 25165824
  22.6 18.1 %copy.67 = f32[2048,2048]{0,1:T(8,128)} copy(f32[2048,2048]{1,0:T(8,128)} %bitcast.95) | data formatting | bytes 33554432 | tf_op jit(solution)/shard_map/convert_element_type | solution.py:62
  47.6 28.0 %all-gather.7.cloned.1.call-done = bf16[1,256,8,1,256]{4,2,3,0,1:T(8,128)(2,1)} async-done(((bf16[1,32,8,1,256]{4,2,3,0,1:T(8,128)(2,1)}), bf16[1,256,8,1,256]{4,2,3,0,1:T(8,128)(2,1)}) %all-gather.7.cloned.1.call-update) | async-done | bytes 1048592 | tf_op jit(solution)/shard_map/all_gather | solution.py:54
  96.8 12.6 %copy.58 = bf16[8,256,8,256]{3,1,2,0:T(8,128)(2,1)} copy(bf16[8,256,8,256]{1,0,3,2:T(8,128)(2,1)} %bitcast.101) | data formatting | bytes 16777216 | tf_op jit(solution)/shard_map/reshape | solution.py:64
  124.8 10.7 %gather_fusion.3 = bf16[16,8,256,256]{3,2,1,0:T(8,128)(2,1)} fusion(bf16[8,256,8,256]{3,1,2,0:T(8,128)(2,1)} %broadcast_select_fusion, s32[1024]{0:T(1024)S(1)} %pad_clamp_fusion.4), kind=kCustom, calls=%fused_computation.11 | custom fusion | bytes 33554496 | tf_op jit(solution)/shard_map/jit(_take)/gather | solution.py:100
  146.6 188.0 %all_to_all.15 = bf16[8,256,16,256]{3,1,2,0:T(8,128)(2,1)} all-to-all(bf16[8,256,16,256]{3,1,2,0:T(8,128)(2,1)S(1)} %copy.59), channel_id=1, replica_groups=mesh['half'=2,'row'=8,'col'=8] {'row'}, dimensions={0} | all-to-all | bytes 33554432 | tf_op jit(solution)/shard_map/all_to_all | solution.py:102
  343.3 14.0 %copy.60 = bf16[8,256,16,256]{3,1,0,2:T(8,128)(2,1)} copy(bf16[8,256,16,256]{3,1,2,0:T(8,128)(2,1)} %all_to_all.15) | data formatting | bytes 33554432 | tf_op jit(solution)/shard_map/all_to_all | solution.py:102
  357.3 14.5 %all-to-all-done = bf16[16,16,16,1,256]{4,2,1,3,0:T(8,128)(2,1)S(1)} async-done(((bf16[16,16,16,1,256]{4,2,1,3,0:T(8,128)(2,1)}), bf16[16,16,16,1,256]{4,2,1,3,0:T(8,128)(2,1)S(1)}, u32[]{:S(2)}, u32[]{:S(2)}) %all-to-all-start) | async-done | bytes 2097184 | tf_op jit(solution)/shard_map/all_to_all | solution.py:75
  380.9 11.4 %broadcast_multiply_fusion = f32[16,256,8,256]{1,0,3,2:T(8,128)} fusion(f32[256,256]{0,1:T(8,128)S(1)} %fusion.2, f32[16,256,8]{1,0,2:T(8,128)S(1)} %broadcast_multiply_fusion.1), kind=kLoop, calls=%fused_computation.24 | loop fusion | flops 8388608 | bytes 33947648 | tf_op jit(solution)/shard_map/mul | solution.py:72
  394.3 37.9 %copy.71 = f32[256,8,16,256]{3,1,2,0:T(8,128)} copy(f32[256,8,16,256]{3,2,1,0:T(8,128)} %bitcast.93) | data formatting | bytes 67108864
  435.5 85.6 %all-gather.5.cloned.1.call-done = bf16[256,8,1,256]{3,1,2,0:T(8,128)(2,1)} async-done(((bf16[32,8,1,256]{3,1,2,0:T(8,128)(2,1)}), bf16[256,8,1,256]{3,1,2,0:T(8,128)(2,1)}) %all-gather.5.cloned.1.call-update) | async-done | bytes 1048592 | tf_op jit(solution)/shard_map/all_gather | solution.py:43
  525.1 21.5 %bitcast_subtract_fusion = f32[4096,2048]{0,1:T(8,128)} fusion(f32[4096,2048]{0,1:T(8,128)} %bitcast.91, bf16[256,4096]{1,0:T(8,128)(2,1)S(1)} %bitcast.103, bf16[256,256]{1,0:T(8,128)(2,1)S(1)} %copy-done, bf16[256,2048]{1,0:T(8,128)(2,1)S(1)} %bitcast.105), kind=kOutput, calls=%fused_computation.16 | convolution fusion | flops 4572315648 | bytes 70385664 | tf_op jit(solution)/shard_map/dot_general | solution.py:83
  546.6 30.2 %copy.74 = f32[256,8,16,256]{3,2,1,0:T(8,128)} copy(f32[256,8,16,256]{3,1,2,0:T(8,128)} %bitcast.92) | data formatting | bytes 67108864
  576.7 34.6 %copy.63 = f32[16,256,8,256]{3,1,0,2:T(8,128)} copy(f32[16,256,8,256]{1,0,3,2:T(8,128)} %bitcast.94) | data formatting | bytes 67108864 | tf_op jit(solution)/shard_map/reshape | solution.py:108
  611.3 12.0 %fusion.18 = (bf16[8,128,16,256]{3,1,0,2:T(8,128)(2,1)}, bf16[8,128,16,256]{3,1,0,2:T(8,128)(2,1)}) fusion(bf16[8,256,16,256]{3,1,0,2:T(8,128)(2,1)} %all-to-all-done.2), kind=kLoop, calls=%fused_computation.102 | loop fusion | bytes 33554432 | tf_op jit(solution)/shard_map/jit(_take)/gather | solution.py:106
  638.7 10.5 %gather_fusion.11 = bf16[16,128,16,256]{3,1,2,0:T(8,128)(2,1)} fusion(bf16[8,128,16,256]{3,1,2,0:T(8,128)(2,1)} %copy.70, s32[1024]{0:T(1024)S(1)} %pad_clamp_fusion.1), kind=kCustom, calls=%fused_computation.5.clone | custom fusion | bytes 33554496 | tf_op jit(solution)/shard_map/jit(_take)/gather | solution.py:106
  649.2 10.6 %gather_fusion.7 = bf16[16,128,16,256]{3,1,2,0:T(8,128)(2,1)} fusion(bf16[8,128,16,256]{3,1,2,0:T(8,128)(2,1)} %copy.70, s32[1024]{0:T(1024)S(1)} %pad_clamp_fusion.3), kind=kCustom, calls=%fused_computation.1.clone | custom fusion | bytes 33554496 | tf_op jit(solution)/shard_map/jit(_take)/gather | solution.py:106
  680.7 22.7 %maximum_select_fusion = bf16[16,256,16,256]{3,1,2,0:T(8,128)(2,1)} fusion(bf16[16,128,16,256]{3,1,2,0:T(8,128)(2,1)} %gather_fusion.7, bf16[16,128,16,256]{3,1,2,0:T(8,128)(2,1)} %gather_fusion.6, pred[16]{0:T(512)(128)(4,1)S(1)} %get-tuple-element.39), kind=kLoop, calls=%fused_computation.14 | loop fusion | flops 83886080 | bytes 67108880 | tf_op jit(solution)/shard_map/jit(_take)/select_n | solution.py:106
  703.4 23.3 %fusion.17 = (bf16[16,128,16,256]{3,1,2,0:T(8,128)(2,1)}, bf16[16,128,16,256]{3,1,2,0:T(8,128)(2,1)}) fusion(bf16[16,256,16,256]{3,1,2,0:T(8,128)(2,1)} %maximum_select_fusion), kind=kLoop, calls=%fused_computation.101 | loop fusion | bytes 67108864 | tf_op jit(solution)/shard_map/jit(_take)/gather | solution.py:107
  747.5 22.7 %maximum_select_fusion.1 = bf16[16,256,16,256]{3,1,2,0:T(8,128)(2,1)} fusion(bf16[16,128,16,256]{3,1,2,0:T(8,128)(2,1)} %gather_fusion.11, bf16[16,128,16,256]{3,1,2,0:T(8,128)(2,1)} %gather_fusion.10, pred[16]{0:T(512)(128)(4,1)S(1)} %copy-done.11), kind=kLoop, calls=%fused_computation.15 | loop fusion | flops 83886080 | bytes 67108880 | tf_op jit(solution)/shard_map/jit(_take)/select_n | solution.py:106
  770.1 23.3 %fusion.16 = (bf16[16,128,16,256]{3,1,2,0:T(8,128)(2,1)}, bf16[16,128,16,256]{3,1,2,0:T(8,128)(2,1)}) fusion(bf16[16,256,16,256]{3,1,2,0:T(8,128)(2,1)} %maximum_select_fusion.1), kind=kLoop, calls=%fused_computation.100 | loop fusion | bytes 67108864 | tf_op jit(solution)/shard_map/jit(_take)/gather | solution.py:107
  803.8 10.5 %gather_fusion.13 = bf16[8,16,128,256]{3,2,1,0:T(8,128)(2,1)} fusion(bf16[16,128,16,256]{3,1,2,0:T(8,128)(2,1)} %get-tuple-element.25, s32[1024]{0:T(1024)} %pad_clamp_fusion), kind=kCustom, calls=%fused_computation.7.clone | custom fusion | bytes 16777248 | tf_op jit(solution)/shard_map/jit(_take)/gather | solution.py:107
  814.4 22.2 %fusion = bf16[16,1,256,8,1,256]{5,2,0,3,4,1:T(8,128)(2,1)S(1)} fusion(f32[16,256,8,256]{3,1,0,2:T(8,128)} %copy.63, bf16[16,128,8,256]{3,1,0,2:T(8,128)(2,1)} %bitcast.97, bf16[16,128,8,256]{3,1,0,2:T(8,128)(2,1)} %bitcast.96, bf16[16,128,8,256]{3,1,0,2:T(8,128)(2,1)} %bitcast.99, bf16[16,128,8,256]{3,1,0,2:T(8,128)(2,1)} %bitcast.98, ...), kind=kLoop, calls=%fused_computation.18 | loop fusion | flops 142606336 | bytes 83886352 | tf_op jit(solution)/shard_map/reshape | solution.py:115
  836.6 11.1 %copy.66 = bf16[16,1,256,8,1,256]{5,3,4,2,1,0:T(8,128)(2,1)} copy(bf16[16,1,256,8,1,256]{5,2,0,3,4,1:T(8,128)(2,1)S(1)} %fusion) | data formatting | bytes 33554432 | tf_op jit(solution)/shard_map/reshape | solution.py:115
  (99 shorter events, 151.1 us)
Async XLA Ops:
  6.5 518.5 %copy-start = (bf16[256,256]{1,0:T(8,128)(2,1)S(1)}, bf16[256,256]{1,0:T(8,128)(2,1)}, u32[]{:S(2)}) copy-start(bf16[256,256]{1,0:T(8,128)(2,1)} %param.20) | copy-start | bytes 393220
  6.5 39.5 %all-gather.9.cloned.1.call-start = ((), (), s32[]{:S(2)}) async-start(), calls=%async_computation.5 | async-start | bytes 1179648 | tf_op jit(solution)/shard_map/all_gather | solution.py:42
  7.3 68.4 %all-gather.7.cloned.1.call-start = ((), (), s32[]{:S(2)}) async-start(), calls=%async_computation.4 | async-start | bytes 1179648 | tf_op jit(solution)/shard_map/all_gather | solution.py:54
  22.6 54.6 %copy-start.3 = (bf16[1,256,256]{2,1,0:T(8,128)(2,1)S(1)}, bf16[1,256,256]{2,1,0:T(8,128)(2,1)}, u32[]{:S(2)}) copy-start(bf16[1,256,256]{2,1,0:T(8,128)(2,1)} %param.16) | copy-start | bytes 393220
  146.5 188.0 %copy-start.4 = (bf16[16,16,1,256]{3,1,2,0:T(8,128)(2,1)S(1)}, bf16[16,16,1,256]{3,1,2,0:T(8,128)(2,1)}, u32[]{:S(2)}) copy-start(bf16[16,16,1,256]{3,1,2,0:T(8,128)(2,1)} %param.19) | copy-start | bytes 393220
  336.1 35.7 %all-to-all-start = ((bf16[16,16,16,1,256]{4,2,1,3,0:T(8,128)(2,1)}), bf16[16,16,16,1,256]{4,2,1,3,0:T(8,128)(2,1)S(1)}, u32[]{:S(2)}, u32[]{:S(2)}) async-start(bf16[16,16,16,1,256]{4,2,1,3,0:T(8,128)(2,1)} %stack.2), calls=%async_computation | async-start | bytes 4194304 | tf_op jit(solution)/shard_map/all_to_all | solution.py:75
  357.3 22.2 %copy-start.5 = (f32[16,1,256]{2,1,0:T(1,128)S(1)}, f32[16,1,256]{2,1,0:T(1,128)}, u32[]{:S(2)}) copy-start(f32[16,1,256]{2,1,0:T(1,128)} %param.21) | copy-start | bytes 49156
  357.3 22.3 %copy-start.8 = (s32[2,64]{1,0:T(2,128)S(1)}, s32[2,64]{1,0:T(2,128)}, u32[]{:S(2)}) copy-start(s32[2,64]{1,0:T(2,128)} %param.17) | copy-start | bytes 1540
  371.8 1.3 copy-start.2
  373.1 238.2 %all-to-all-start.2 = ((bf16[8,256,16,256]{3,1,0,2:T(8,128)(2,1)}), bf16[8,256,16,256]{3,1,0,2:T(8,128)(2,1)}, u32[]{:S(2)}, u32[]{:S(2)}) async-start(bf16[8,256,16,256]{3,1,0,2:T(8,128)(2,1)} %copy.60), calls=%async_computation.2 | async-start | bytes 33554432 | tf_op jit(solution)/shard_map/all_to_all | solution.py:103
  378.8 142.2 %all-gather.5.cloned.1.call-start = ((), (), s32[]{:S(2)}) async-start(), calls=%async_computation.3 | async-start | bytes 1179648 | tf_op jit(solution)/shard_map/all_gather | solution.py:43
  726.7 20.8 %copy-start.11 = (pred[16]{0:T(512)(128)(4,1)S(1)}, pred[16]{0:T(512)(128)(4,1)}, u32[]{:S(2)}) copy-start(pred[16]{0:T(512)(128)(4,1)} %get-tuple-element.38) | copy-start | bytes 52
  793.5 20.9 %copy-start.6 = (pred[16,8]{0,1:T(8,128)(4,1)S(1)}, pred[16,8]{0,1:T(8,128)(4,1)}, u32[]{:S(2)}) copy-start(pred[16,8]{0,1:T(8,128)(4,1)} %get-tuple-element.30) | copy-start | bytes 388
  793.5 20.9 %copy-start.7 = (pred[16,8]{0,1:T(8,128)(4,1)S(1)}, pred[16,8]{0,1:T(8,128)(4,1)}, u32[]{:S(2)}) copy-start(pred[16,8]{0,1:T(8,128)(4,1)} %get-tuple-element.31) | copy-start | bytes 388
  793.5 20.9 %copy-start.9 = (pred[8]{0:T(512)(128)(4,1)S(1)}, pred[8]{0:T(512)(128)(4,1)}, u32[]{:S(2)}) copy-start(pred[8]{0:T(512)(128)(4,1)} %get-tuple-element.36) | copy-start | bytes 28
  793.5 20.9 %copy-start.10 = (pred[8]{0:T(512)(128)(4,1)S(1)}, pred[8]{0:T(512)(128)(4,1)}, u32[]{:S(2)}) copy-start(pred[8]{0:T(512)(128)(4,1)} %get-tuple-element.37) | copy-start | bytes 28
  814.4 33.3 %copy-start.1 = (bf16[256,256]{1,0:T(8,128)(2,1)S(1)}, bf16[256,256]{1,0:T(8,128)(2,1)}, u32[]{:S(2)}) copy-start(bf16[256,256]{1,0:T(8,128)(2,1)} %param.20) | copy-start | bytes 393220
Sparse Core Ops, SparseCore 0:
  9.0 37.0 all-gather.8
  47.8 27.8 all-gather.6
  381.2 139.7 all-gather.4
